TPU v7x, 32 devices: a whole 2x2x4 slice. The times are simulated.
32 devices in a mesh: dp: 2 (over x), row: 4 (over y, core), col: 4 (over z).
Axes of the slice: x: 2, y: 2, z: 4, core: 2. Of those that a mesh axis runs over, the one named last changes fastest.
Arguments:
- tokens: bfloat16 [768, 39200], P('row', ('dp', 'col')), may hold values from -6 to 6
- grad_out: bfloat16 [768, 39200], P('row', ('dp', 'col')), may hold values from -6 to 6
- adapter_index: int32 [8, 1], replicated, may hold values from 0 to 7
- norm1_gain: bfloat16 [768], P('row'), may hold values from 0.099609375 to 1.8984375
- norm2_gain: bfloat16 [768], P('row'), may hold values from 0.099609375 to 1.8984375
- qkv_weight: bfloat16 [768, 2304], P('row', 'col'), may hold values from -0.21875 to 0.21875
- proj_weight: bfloat16 [768, 768], P('col', 'row'), may hold values from -0.875 to 0.875
- fc1_weight: bfloat16 [768, 3072], P('row', 'col'), may hold values from -0.21875 to 0.21875
- fc2_weight: bfloat16 [768, 3072], P('row', 'col'), may hold values from -0.109375 to 0.109375
- rel_h: bfloat16 [27, 64], replicated, may hold values from -0.59765625 to 0.59765625
- rel_w: bfloat16 [27, 64], replicated, may hold values from -0.59765625 to 0.59765625
- qkv_down: bfloat16 [8, 768, 16], P(None, 'row'), may hold values from -0.21875 to 0.21875
- qkv_up: bfloat16 [8, 16, 2304], P(None, None, 'col'), may hold values from -0.75 to 0.75
- proj_down: bfloat16 [8, 768, 16], P(None, 'col'), may hold values from -0.21875 to 0.21875
- proj_up: bfloat16 [8, 16, 768], P(None, None, 'row'), may hold values from -0.75 to 0.75
- fc1_down: bfloat16 [8, 768, 16], P(None, 'row'), may hold values from -0.21875 to 0.21875
- fc1_up: bfloat16 [8, 16, 3072], P(None, None, 'col'), may hold values from -0.75 to 0.75
- fc2_down: bfloat16 [8, 3072, 16], P(None, 'col'), may hold values from -0.109375 to 0.109375
- fc2_up: bfloat16 [8, 16, 768], P(None, None, 'row'), may hold values from -0.75 to 0.75
Outputs:
- out: bfloat16 [768, 39200], P('row', ('dp', 'col'))
- tokens_grad: float32 [768, 39200], P('row', ('dp', 'col'))
- qkv_down_grad: float32 [8, 768, 16], P(None, 'row')
- qkv_up_grad: float32 [8, 16, 2304], P(None, None, 'col')
- proj_down_grad: float32 [8, 768, 16], P(None, 'col')
- proj_up_grad: float32 [8, 16, 768], P(None, None, 'row')
- fc1_down_grad: float32 [8, 768, 16], P(None, 'row')
- fc1_up_grad: float32 [8, 16, 3072], P(None, None, 'col')
- fc2_down_grad: float32 [8, 3072, 16], P(None, 'col')
- fc2_up_grad: float32 [8, 16, 768], P(None, None, 'row')
Inputs may be any that keep to these rules, and one draw needn't show every extreme that they name: `adapter_index`: every one of the 8 adapters is chosen by at least one image.
All inputs are finite; a program needn't handle non-finite values.
Results may differ from a plain program's by a relative error of at most 0.015.
Values may be sent and summed in bfloat16 or wider, within the bound.
No kernel may reach another device: no remote copies, remote signals or barrier semaphores. Data moves between devices by JAX's collectives and lax.ppermute only.
A program may use at most 448 MiB of HBM per device.

v0:
```python
import jax
import jax.numpy as jnp
from jax import lax
from jax.sharding import PartitionSpec as P

D = 768
HD = 64
WIN = 14
SIDE = 64
ADAPT = 8
NWIN_SIDE = 5
IMG_TOK = 4900
PRECISE = lax.Precision.HIGHEST
EPSILON = 1e-06


def exact_gelu(values):
    return jax.nn.gelu(values, approximate=False)


def valid_rows():
    position = jnp.arange(IMG_TOK, dtype=jnp.int32)
    window = position // (WIN * WIN)
    inside = position % (WIN * WIN)
    image_row = window // NWIN_SIDE * WIN + inside // WIN
    image_col = window % NWIN_SIDE * WIN + inside % WIN
    return ((image_row < SIDE) & (image_col < SIDE)).astype(jnp.float32)


def rel_table(rel_param):
    offsets = (
        jnp.arange(WIN, dtype=jnp.int32)[:, None]
        - jnp.arange(WIN, dtype=jnp.int32)[None, :]
        + WIN
        - 1
    )
    one_hot = (
        offsets[:, :, None] == jnp.arange(2 * WIN - 1, dtype=jnp.int32)[None, None, :]
    ).astype(jnp.bfloat16)
    return jnp.einsum("akn,nc->akc", one_hot, rel_param, preferred_element_type=jnp.float32).astype(
        jnp.bfloat16
    )


def pick_one(adapter, own_pick):
    return jnp.einsum("a,ade->de", own_pick, adapter.astype(jnp.float32), precision=PRECISE).astype(
        jnp.bfloat16
    )


def row_totals(first_sum, second_sum):
    return lax.psum((first_sum, second_sum), "row")


def norm_forward(values):
    totals = row_totals(jnp.sum(values, axis=1), jnp.sum(values * values, axis=1))
    center = totals[0] / D
    inv_std = lax.rsqrt(totals[1] / D - center * center + EPSILON)
    return ((values - center[:, None]) * inv_std[:, None], inv_std)


def norm_backward(grad_normed, normed, inv_std):
    totals = row_totals(jnp.sum(grad_normed, axis=1), jnp.sum(grad_normed * normed, axis=1))
    return inv_std[:, None] * (
        grad_normed - totals[0][:, None] / D - normed * totals[1][:, None] / D
    )


def local_norm(values):
    center = jnp.sum(values, axis=1) / D
    inv_std = lax.rsqrt(jnp.sum(values * values, axis=1) / D - center * center + EPSILON)
    return ((values - center[:, None]) * inv_std[:, None], inv_std)


def local_norm_back(grad_normed, normed, inv_std):
    first_mean = jnp.sum(grad_normed, axis=1) / D
    second_mean = jnp.sum(grad_normed * normed, axis=1) / D
    return inv_std[:, None] * (grad_normed - first_mean[:, None] - normed * second_mean[:, None])


def to_features(values):
    return lax.all_to_all(
        values.astype(jnp.bfloat16), "row", split_axis=0, concat_axis=1, tiled=True
    ).astype(values.dtype)


def to_tokens(values):
    return lax.all_to_all(
        values.astype(jnp.bfloat16), "row", split_axis=1, concat_axis=0, tiled=True
    ).astype(values.dtype)


def token_rows(values):
    return lax.all_to_all(values, "row", split_axis=0, concat_axis=1, tiled=True)


def head_cols(values):
    return lax.all_to_all(values, "row", split_axis=1, concat_axis=0, tiled=True)


def head_sums(values):
    return lax.all_to_all(
        values.astype(jnp.bfloat16), "row", split_axis=1, concat_axis=0, tiled=True
    ).astype(values.dtype)


def adapted_local(inputs, weight, down_mat, up_mat):
    product = jnp.dot(inputs, weight, preferred_element_type=jnp.float32)
    reduced = jnp.dot(inputs, down_mat, preferred_element_type=jnp.float32)
    return product + jnp.dot(reduced, up_mat.astype(jnp.float32), precision=PRECISE)


def adapted_back(grads, weight, down_mat, up_mat):
    contract = (((1,), (1,)), ((), ()))
    product = lax.dot_general(grads, weight, contract, preferred_element_type=jnp.float32)
    reduced = lax.dot_general(grads, up_mat, contract, preferred_element_type=jnp.float32)
    return product + lax.dot_general(
        reduced, down_mat.astype(jnp.float32), contract, precision=PRECISE
    )


def pair_grads(inputs_m, grads_m, down_m, up_m):
    reduced = jnp.dot(inputs_m, down_m, preferred_element_type=jnp.float32)
    back_red = lax.dot_general(
        grads_m, up_m, (((1,), (1,)), ((), ())), preferred_element_type=jnp.float32
    )
    grad_down = jnp.einsum("td,tr->dr", inputs_m, back_red, precision=PRECISE)
    grad_up = jnp.einsum("tr,to->ro", reduced, grads_m, precision=PRECISE)
    return (grad_down, grad_up)


def spread_pick(own_pick, grad_mat):
    return jnp.einsum("a,de->ade", own_pick, grad_mat)


def take_block(full, dim, index, length):
    return lax.dynamic_slice_in_dim(full, index * length, length, dim)


def split_qkv(qkv_low):
    heads_local = qkv_low.shape[1] // (3 * HD)
    arranged = qkv_low.reshape(NWIN_SIDE * NWIN_SIDE, WIN * WIN, heads_local, 3, HD)
    return (arranged[:, :, :, 0], arranged[:, :, :, 1], arranged[:, :, :, 2])


def score_matrix(query_b, key_b, tables):
    windows = query_b.shape[0]
    heads_local = query_b.shape[2]
    dot_scores = jnp.einsum(
        "nqhc,nkhc->nhqk", query_b, key_b, preferred_element_type=jnp.float32
    ) * HD ** (-0.5)
    spatial = query_b.reshape(windows, WIN, WIN, heads_local, HD)
    rel_rows = jnp.einsum(
        "nabhc,akc->nhabk", spatial, tables[0], preferred_element_type=jnp.float32
    )
    rel_cols = jnp.einsum(
        "nabhc,bkc->nhabk", spatial, tables[1], preferred_element_type=jnp.float32
    )
    shaped = dot_scores.reshape(windows, heads_local, WIN, WIN, WIN, WIN)
    shaped = shaped + rel_rows[:, :, :, :, :, None] + rel_cols[:, :, :, :, None, :]
    return shaped.reshape(windows, heads_local, WIN * WIN, WIN * WIN)


def attend(qkv_low, tables):
    query_b, key_b, value_b = split_qkv(qkv_low)
    scores = score_matrix(query_b, key_b, tables)
    maxima = jnp.max(scores, axis=3, keepdims=True)
    exponent = jnp.exp(scores - maxima)
    sum_exp = jnp.sum(exponent, axis=3, keepdims=True)
    attn_prob = (exponent / sum_exp).astype(jnp.bfloat16)
    attended = jnp.einsum("nhqk,nkhc->nqhc", attn_prob, value_b, preferred_element_type=jnp.float32)
    log_total = (maxima + jnp.log(sum_exp))[:, :, :, 0]
    return (attended.reshape(IMG_TOK, attended.shape[2] * HD).astype(jnp.bfloat16), log_total)


def attend_back(qkv_low, log_total, grad_attended, tables):
    query_b, key_b, value_b = split_qkv(qkv_low)
    windows = query_b.shape[0]
    heads_local = query_b.shape[2]
    scores = score_matrix(query_b, key_b, tables)
    attn_exact = jnp.exp(scores - log_total[:, :, :, None])
    prob_low = attn_exact.astype(jnp.bfloat16)
    grad_o = grad_attended.reshape(windows, WIN * WIN, heads_local, HD)
    grad_v = jnp.einsum("nhqk,nqhc->nkhc", prob_low, grad_o, preferred_element_type=jnp.float32)
    grad_p = jnp.einsum("nqhc,nkhc->nhqk", grad_o, value_b, preferred_element_type=jnp.float32)
    centre = jnp.sum(grad_p * attn_exact, axis=3, keepdims=True)
    grad_s = (attn_exact * (grad_p - centre)).astype(jnp.bfloat16)
    grad_q = jnp.einsum(
        "nhqk,nkhc->nqhc", grad_s, key_b, preferred_element_type=jnp.float32
    ) * HD ** (-0.5)
    grad_k = jnp.einsum(
        "nhqk,nqhc->nkhc", grad_s, query_b, preferred_element_type=jnp.float32
    ) * HD ** (-0.5)
    split_grad = grad_s.astype(jnp.float32).reshape(windows, heads_local, WIN, WIN, WIN, WIN)
    along_rows = jnp.sum(split_grad, axis=5)
    along_cols = jnp.sum(split_grad, axis=4)
    rel_grad = jnp.einsum(
        "nhabk,akc->nabhc", along_rows, tables[0].astype(jnp.float32), precision=PRECISE
    )
    rel_grad = rel_grad + jnp.einsum(
        "nhabk,bkc->nabhc", along_cols, tables[1].astype(jnp.float32), precision=PRECISE
    )
    grad_q = grad_q + rel_grad.reshape(windows, WIN * WIN, heads_local, HD)
    stacked = jnp.stack([grad_q, grad_k, grad_v], axis=3)
    return stacked.reshape(IMG_TOK, heads_local * 3 * HD).astype(jnp.bfloat16)


def body(
    tokens,
    grad_out,
    adapter_index,
    norm1_gain,
    norm2_gain,
    qkv_weight,
    proj_weight,
    fc1_weight,
    fc2_weight,
    rel_h,
    rel_w,
    qkv_down,
    qkv_up,
    proj_down,
    proj_up,
    fc1_down,
    fc1_up,
    fc2_down,
    fc2_up,
):
    members = lax.axis_size("col")
    row_index = lax.axis_index("row")
    col_index = lax.axis_index("col")
    group_ids = lax.dynamic_slice_in_dim(
        adapter_index[:, 0], lax.axis_index("dp") * members, members, 0
    )
    chosen = (group_ids[:, None] == jnp.arange(ADAPT, dtype=jnp.int32)[None, :]).astype(jnp.float32)
    own_pick = chosen[col_index]
    validity = valid_rows()[:, None]
    tables = (rel_table(rel_h), rel_table(rel_w))
    inputs = tokens.astype(jnp.float32).T
    normed_one, inv_one = norm_forward(inputs)
    gain_one = norm1_gain.astype(jnp.float32)
    hidden_one = (normed_one * gain_one * validity).astype(jnp.bfloat16)
    qkv_part, proj_part, qkv_dn_part, proj_up_part = (
        lax.all_gather(qkv_weight, "row", axis=0, tiled=True),
        lax.all_gather(proj_weight, "row", axis=1, tiled=True),
        lax.all_gather(qkv_down, "row", axis=1, tiled=True),
        lax.all_gather(proj_up, "row", axis=2, tiled=True),
    )
    qkv_full, proj_full, qkv_up_all, proj_dn_all = (
        lax.all_gather(qkv_part, "col", axis=1, tiled=True),
        lax.all_gather(proj_part, "col", axis=0, tiled=True),
        lax.all_gather(qkv_up, "col", axis=2, tiled=True),
        lax.all_gather(proj_down, "col", axis=1, tiled=True),
    )
    qkv_dn = pick_one(qkv_dn_part, own_pick)
    qkv_upm = pick_one(qkv_up_all, own_pick)
    proj_dn = pick_one(proj_dn_all, own_pick)
    proj_upm = pick_one(proj_up_part, own_pick)
    hidden_rows = token_rows(hidden_one)
    qkv_rows_out = adapted_local(hidden_rows, qkv_full, qkv_dn, qkv_upm).astype(jnp.bfloat16)
    qkv_low = head_cols(qkv_rows_out)
    attended, log_total = attend(qkv_low, tables)
    attended_rows = token_rows(attended)
    branch = head_sums(adapted_local(attended_rows, proj_full, proj_dn, proj_upm))
    middle = inputs + branch
    grad_final = grad_out.astype(jnp.float32).T * validity
    weight_up, weight_stored, down_one, up_two, gain_full = (
        lax.all_gather(fc1_weight, "row", axis=0, tiled=True),
        lax.all_gather(fc2_weight, "row", axis=0, tiled=True),
        lax.all_gather(fc1_down, "row", axis=1, tiled=True),
        lax.all_gather(fc2_up, "row", axis=2, tiled=True),
        lax.all_gather(norm2_gain, "row", axis=0, tiled=True),
    )
    weight_up, weight_stored, up_one, down_two = (
        lax.all_gather(weight_up, "col", axis=1, tiled=True),
        lax.all_gather(weight_stored, "col", axis=1, tiled=True),
        lax.all_gather(fc1_up, "col", axis=2, tiled=True),
        lax.all_gather(fc2_down, "col", axis=1, tiled=True),
    )
    weight_down = weight_stored.T
    down_fc1 = pick_one(down_one, own_pick)
    up_fc1 = pick_one(up_one, own_pick)
    down_fc2 = pick_one(down_two, own_pick)
    up_fc2 = pick_one(up_two, own_pick)
    local_mid = to_features(middle)
    normed_two, inv_two = local_norm(local_mid)
    gain_two = gain_full.astype(jnp.float32)
    hidden_two = (normed_two * gain_two).astype(jnp.bfloat16)
    pre_act = adapted_local(hidden_two, weight_up, down_fc1, up_fc1)
    activated = exact_gelu(pre_act).astype(jnp.bfloat16)
    mlp_out = to_tokens(adapted_local(activated, weight_down, down_fc2, up_fc2))
    grad_local = to_features(grad_final).astype(jnp.bfloat16)
    grad_activ = adapted_back(grad_local, weight_down, down_fc2, up_fc2)
    gelu_value, gelu_back = jax.vjp(exact_gelu, pre_act)
    grad_pre = gelu_back(grad_activ)[0].astype(jnp.bfloat16)
    grad_hidden_two = adapted_back(grad_pre, weight_up, down_fc1, up_fc1)
    grad_middle = grad_final + to_tokens(
        local_norm_back(grad_hidden_two * gain_two, normed_two, inv_two)
    )
    fc1_local = pair_grads(hidden_two, grad_pre, down_fc1, up_fc1)
    fc2_local = pair_grads(activated, grad_local, down_fc2, up_fc2)
    summed_all = lax.psum(
        (
            spread_pick(own_pick, fc1_local[0]),
            spread_pick(own_pick, fc1_local[1]),
            spread_pick(own_pick, fc2_local[0]),
            spread_pick(own_pick, fc2_local[1]),
        ),
        ("dp", "row", "col"),
    )
    fc1_down_grad = take_block(summed_all[0], 1, row_index, fc1_down.shape[1])
    fc1_up_grad = take_block(summed_all[1], 2, col_index, fc1_up.shape[2])
    fc2_down_grad = take_block(summed_all[2], 1, col_index, fc2_down.shape[1])
    fc2_up_grad = take_block(summed_all[3], 2, row_index, fc2_up.shape[2])
    result = ((middle + mlp_out) * validity).astype(jnp.bfloat16).T
    grad_branch = grad_middle.astype(jnp.bfloat16)
    grad_branch_rows = token_rows(grad_branch)
    grad_attended = head_cols(
        adapted_back(grad_branch_rows, proj_full, proj_dn, proj_upm).astype(jnp.bfloat16)
    )
    grad_qkv = attend_back(qkv_low, log_total, grad_attended, tables)
    grad_qkv_rows = token_rows(grad_qkv)
    grad_hidden_one = head_sums(adapted_back(grad_qkv_rows, qkv_full, qkv_dn, qkv_upm))
    qkv_pair = pair_grads(hidden_rows, grad_qkv_rows, qkv_dn, qkv_upm)
    proj_pair = pair_grads(attended_rows, grad_branch_rows, proj_dn, proj_upm)
    attn_sums = lax.psum(
        (
            spread_pick(own_pick, qkv_pair[0]),
            spread_pick(own_pick, qkv_pair[1]),
            spread_pick(own_pick, proj_pair[0]),
            spread_pick(own_pick, proj_pair[1]),
        ),
        ("dp", "row", "col"),
    )
    qkv_down_grad = take_block(attn_sums[0], 1, row_index, qkv_down.shape[1])
    qkv_up_grad = take_block(attn_sums[1], 2, col_index, qkv_up.shape[2])
    proj_down_grad = take_block(attn_sums[2], 1, col_index, proj_down.shape[1])
    proj_up_grad = take_block(attn_sums[3], 2, row_index, proj_up.shape[2])
    grad_inputs = (
        grad_middle + norm_backward(grad_hidden_one * validity * gain_one, normed_one, inv_one)
    ).T
    return (
        result,
        grad_inputs,
        qkv_down_grad,
        qkv_up_grad,
        proj_down_grad,
        proj_up_grad,
        fc1_down_grad,
        fc1_up_grad,
        fc2_down_grad,
        fc2_up_grad,
    )


def solution(mesh):
    return jax.shard_map(
        body,
        mesh=mesh,
        in_specs=(
            P("row", ("dp", "col")),
            P("row", ("dp", "col")),
            P(),
            P("row"),
            P("row"),
            P("row", "col"),
            P("col", "row"),
            P("row", "col"),
            P("row", "col"),
            P(),
            P(),
            P(None, "row", None),
            P(None, None, "col"),
            P(None, "col", None),
            P(None, None, "row"),
            P(None, "row", None),
            P(None, None, "col"),
            P(None, "col", None),
            P(None, None, "row"),
        ),
        out_specs=(
            P("row", ("dp", "col")),
            P("row", ("dp", "col")),
            P(None, "row", None),
            P(None, None, "col"),
            P(None, "col", None),
            P(None, None, "row"),
            P(None, "row", None),
            P(None, None, "col"),
            P(None, "col", None),
            P(None, None, "row"),
        ),
        check_vma=False,
    )
```

profile of v0, /device:TPU:0, one launch (start us, length us, event | category | flops | bytes accessed | tf_op | source)
XLA Modules:
  0.0 1826.9 jit_solution(15166732212104624496)
XLA Ops:
  46.7 118.0 %all_gather.54 = bf16[8,16,2304]{1,0,2:T(8,128)(2,1)} all-gather(bf16[8,16,576]{1,0,2:T(8,128)(2,1)S(1)} %copy.225), channel_id=1, replica_groups=mesh['dp'=2,'row'=4,'col'=4] {'col'}, dimensions={2}, use_global_device_ids=true | all-gather | bytes 737280 | tf_op jit(solution)/shard_map/all_gather | solution.py:252
  171.6 12.9 all_gather.62
  184.5 30.9 %all_gather.57 = bf16[8,768,16]{2,0,1:T(8,128)(2,1)S(1)} all-gather(bf16[8,192,16]{2,0,1:T(8,128)(2,1)} %copy.243), channel_id=1, replica_groups=mesh['dp'=2,'row'=4,'col'=4] {'col'}, dimensions={1}, use_global_device_ids=true | all-gather | bytes 245760 | tf_op jit(solution)/shard_map/all_gather | solution.py:253
  215.4 12.6 all_gather.53
  263.0 74.5 %all_gather.55 = bf16[192,768]{0,1:T(8,128)(2,1)S(1)} all-gather(bf16[192,192]{0,1:T(8,128)(2,1)S(1)} %copy.241), channel_id=1, replica_groups=mesh['dp'=2,'row'=4,'col'=4] {'row'}, dimensions={1}, use_global_device_ids=true | all-gather | bytes 368640 | tf_op jit(solution)/shard_map/all_gather | solution.py:245
  338.7 13.0 all_gather.58
  372.0 26.8 %reshape.211 = bf16[25,196,3,3,64]{1,0,4,3,2:T(8,128)(2,1)} reshape(bf16[4,1225,576]{1,0,2:T(4,128)(2,1)} %copy.227) | data formatting | bytes 11289600 | tf_op jit(solution)/shard_map/reshape | solution.py:142
  427.1 21.4 %add.271 = f32[25,3,14,14,14,14]{0,5,4,3,2,1:T(8,128)} broadcast(f32[25,3,14,14,14]{0,4,3,2,1:T(8,128)S(1)} %copy.236), dimensions={0,1,2,3,5} | broadcast | bytes 12348000 | tf_op jit(solution)/shard_map/add | solution.py:160
  448.6 64.5 %add.272 = f32[25,3,196,196]{0,3,2,1:T(8,128)} reshape(f32[25,3,14,14,14,14]{0,5,4,3,2,1:T(8,128)} %add.271) | data formatting | bytes 23049600 | tf_op jit(solution)/shard_map/add | solution.py:160
  513.1 39.1 %copy.237 = f32[25,3,196,196]{2,3,1,0:T(8,128)} copy(f32[25,3,196,196]{0,3,2,1:T(8,128)} %add.272) | data formatting | bytes 23049600 | tf_op jit(solution)/shard_map/add | solution.py:160
  563.4 22.8 %add.268 = f32[25,3,14,14,14,14]{0,5,4,3,2,1:T(8,128)} broadcast(f32[25,3,14,14,14]{0,4,3,2,1:T(8,128)} %copy.233), dimensions={0,1,2,3,4} | broadcast | bytes 12348000 | tf_op jit(solution)/shard_map/add | solution.py:160
  586.3 64.5 %add.269 = f32[25,3,196,196]{0,3,2,1:T(8,128)} reshape(f32[25,3,14,14,14,14]{0,5,4,3,2,1:T(8,128)} %add.268) | data formatting | bytes 23049600 | tf_op jit(solution)/shard_map/add | solution.py:160
  650.8 39.1 %copy.234 = f32[25,3,196,196]{2,3,1,0:T(8,128)} copy(f32[25,3,196,196]{0,3,2,1:T(8,128)} %add.269) | data formatting | bytes 23049600 | tf_op jit(solution)/shard_map/add | solution.py:160
  689.9 24.5 %fusion.132 = (f32[25,3,196]{2,1,0:T(4,128)S(1)}, f32[25,3,196,196]{2,3,1,0:T(8,128)}) fusion(f32[25,3,196,196]{2,3,1,0:T(8,128)} %copy.237, f32[25,3,196,196]{2,3,1,0:T(8,128)} %copy.234, bf16[25,196,3,1,64]{1,0,4,3,2:T(8,128)(2,1)} %get-tuple-element.37, bf16[25,196,3,1,64]{1,0,4,3,2:T(8,128)(2,1)S(1)} %copy-done.9), kind=kOutput, calls=%fused_computation.234 | convolution fusion | flops 380303744 | bytes 38396400 | tf_op jit(solution)/shard_map/nqhc,nkhc->nhqk/dot_general | solution.py:149
  779.3 33.6 %all_gather.67 = bf16[8,16,768]{1,0,2:T(8,128)(2,1)S(1)} all-gather(bf16[8,16,192]{1,0,2:T(8,128)(2,1)} %copy.250), channel_id=1, replica_groups=mesh['dp'=2,'row'=4,'col'=4] {'row'}, dimensions={2}, use_global_device_ids=true | all-gather | bytes 245760 | tf_op jit(solution)/shard_map/all_gather | solution.py:271
  814.5 19.3 %all_gather.66 = bf16[8,3072,16]{1,2,0:T(8,128)(2,1)S(1)} all-gather(bf16[8,768,16]{1,2,0:T(8,128)(2,1)} %param.36), channel_id=1, replica_groups=mesh['dp'=2,'row'=4,'col'=4] {'col'}, dimensions={1}, use_global_device_ids=true | all-gather | bytes 983040 | tf_op jit(solution)/shard_map/all_gather | solution.py:278
  868.1 30.2 %all_gather.63 = bf16[8,16,3072]{2,1,0:T(8,128)(2,1)S(1)} all-gather(bf16[8,16,768]{2,1,0:T(8,128)(2,1)S(1)} %copy-done.72), channel_id=1, replica_groups=mesh['dp'=2,'row'=4,'col'=4] {'col'}, dimensions={2}, use_global_device_ids=true | all-gather | bytes 983040 | tf_op jit(solution)/shard_map/all_gather | solution.py:277
  928.8 11.8 fusion.137
  940.6 12.5 all-to-all-done.4
  975.9 41.4 %multiply_convert_fusion.1 = (bf16[1225,3072]{1,0:T(8,128)(2,1)}, f32[1225,3072]{1,0:T(8,128)}, f32[1225,3072]{1,0:T(8,128)}) fusion(f32[1225,3072]{1,0:T(8,128)S(1)} %fusion.135, f32[1225,16]{0,1:T(8,128)S(1)} %fusion.149, bf16[1,16,3072]{2,0,1:T(2,128)(2,1)S(1)} %fusion.64), kind=kOutput, calls=%fused_computation.9 | convolution fusion | flops 970905600 | bytes 52861504 | tf_op jit(solution)/shard_map/dot_general | solution.py:110
  1017.3 23.1 %add_convert_fusion = bf16[1225,3072]{1,0:T(8,128)(2,1)} fusion(f32[1225,3072]{1,0:T(8,128)} %get-tuple-element.32, f32[1225,3072]{1,0:T(8,128)} %fusion.137, f32[1225,3072]{1,0:T(8,128)} %get-tuple-element.51, f32[1225,16]{0,1:T(8,128)S(1)} %fusion.116, bf16[1,3072,16]{1,2,0:T(8,128)(2,1)S(1)} %copy.292), kind=kOutput, calls=%fused_computation.8 | convolution fusion | flops 778982400 | bytes 52861504 | tf_op jit(solution)/shard_map/dot_general | solution.py:117
  1062.8 26.9 %all_to_all.186 = bf16[1225,4,192]{0,2,1:T(8,128)(2,1)S(1)} all-to-all(bf16[1225,4,192]{0,2,1:T(8,128)(2,1)S(1)} %bitcast.307), channel_id=1, replica_groups=mesh['dp'=2,'row'=4,'col'=4] {'row'}, dimensions={1} | all-to-all | bytes 3763200 | tf_op jit(solution)/shard_map/all_to_all | solution.py:88
  1114.9 23.5 %all-to-all-done.8 = bf16[4,1225,192]{1,2,0:T(8,128)(2,1)S(1)} async-done(((bf16[4,1225,192]{1,2,0:T(8,128)(2,1)}), bf16[4,1225,192]{1,2,0:T(8,128)(2,1)S(1)}, u32[]{:S(2)}, u32[]{:S(2)}) %all-to-all-start.8) | async-done | bytes 1881632 | tf_op jit(solution)/shard_map/all_to_all | solution.py:94
  1208.2 21.7 %multiply_reduce_fusion = (f32[25,3,196]{2,1,0:T(4,128)S(1)}, f32[25,3,196,196]{2,3,1,0:T(8,128)}) fusion(f32[25,3,196,196]{2,3,1,0:T(8,128)} %get-tuple-element.50, f32[25,3,196]{2,1,0:T(4,128)S(1)} %log_add_fusion, bf16[25,196,3,1,64]{1,0,4,3,2:T(8,128)(2,1)} %get-tuple-element.35, bf16[25,196,3,64]{1,0,3,2:T(8,128)(2,1)S(1)} %reshape.212), kind=kOutput, calls=%fused_computation.2 | convolution fusion | flops 377422528 | bytes 26930400 | tf_op jit(solution)/shard_map/nqhc,nkhc->nhqk/dot_general | solution.py:185
  1249.0 30.3 %copy.261 = f32[25,3,196,196]{0,3,2,1:T(8,128)} copy(bf16[25,3,196,196]{2,3,1,0:T(8,128)(2,1)} %copy-done.2) | data formatting | bytes 17287200 | tf_op jit(solution)/shard_map/reshape | solution.py:194
  1279.4 64.6 %reshape.221 = f32[25,3,14,14,14,14]{0,5,4,3,2,1:T(8,128)} reshape(f32[25,3,196,196]{0,3,2,1:T(8,128)} %copy.261) | data formatting | bytes 23049600 | tf_op jit(solution)/shard_map/reshape | solution.py:194
  1344.0 94.7 %fusion.128 = (f32[25,3,14,14,14]{0,4,3,2,1:T(8,128)}, f32[25,3,14,14,14]{0,4,3,2,1:T(8,128)}) fusion(f32[25,3,14,14,14,14]{0,5,4,3,2,1:T(8,128)} %reshape.221), kind=kLoop, calls=%fused_computation.231 | loop fusion | flops 5350800 | bytes 13171200 | tf_op jit(solution)/shard_map/reduce_sum | solution.py:195
  1494.7 11.8 copy.269
  1506.5 24.2 %convert_element_type.249 = bf16[4,1225,576]{1,0,2:T(4,128)(2,1)} reshape(bf16[25,196,3,3,64]{1,0,4,3,2:T(8,128)(2,1)} %copy.269) | data formatting | bytes 11289600 | tf_op jit(solution)/shard_map/convert_element_type | solution.py:205
  1577.8 31.0 %all-to-all-done.10 = bf16[4,1225,576]{1,2,0:T(8,128)(2,1)} async-done(((bf16[4,1225,576]{1,2,0:T(8,128)(2,1)}), bf16[4,1225,576]{1,2,0:T(8,128)(2,1)}, u32[]{:S(2)}, u32[]{:S(2)}) %all-to-all-start.10) | async-done | bytes 5644832 | tf_op jit(solution)/shard_map/all_to_all | solution.py:94
  1643.2 17.6 all-to-all-done.11
  1699.4 106.6 %all-reduce.6.cloned.1.call-done = (f32[8,768,16]{1,2,0:T(8,128)}, f32[8,16,2304]{2,1,0:T(8,128)}, f32[8,768,16]{1,2,0:T(8,128)}, f32[8,16,768]{2,1,0:T(8,128)},...) async-done(((f32[8,768,16]{1,2,0:T(8,128)}, f32[8,16,2304]{2,1,0:T(8,128)}, f32[8,768,16]{1,2,0:T(8,128)}, ...) | async-done | bytes 6291472 | tf_op jit(solution)/shard_map/psum | solution.py:326
  (386 shorter events, 621.0 us)
Async XLA Ops:
  7.2 354.6 %copy-start = (bf16[27,64]{1,0:T(8,128)(2,1)S(1)}, bf16[27,64]{1,0:T(8,128)(2,1)}, u32[]{:S(2)}) copy-start(bf16[27,64]{1,0:T(8,128)(2,1)} %param.28) | copy-start | bytes 10372
  7.2 225.9 %all-gather.7.cloned.1.call-start = ((), (), s32[]{:S(2)}) async-start(), calls=%async_computation.12 | async-start | bytes 4423680 | tf_op jit(solution)/shard_map/all_gather | solution.py:250
  41.5 191.2 %all-to-all-start = ((bf16[4,1225,192]{1,2,0:T(8,128)(2,1)}), bf16[4,1225,192]{1,2,0:T(8,128)(2,1)S(1)}, u32[]{:S(2)}, u32[]{:S(2)}) async-start(bf16[4,1225,192]{1,2,0:T(8,128)(2,1)} %copy.222), calls=%async_computation | async-start | bytes 3932160 | tf_op jit(solution)/shard_map/all_to_all | solution.py:94
  45.1 119.6 %copy-start.76 = (bf16[8,192,16]{1,2,0:T(8,128)(2,1)S(1)}, bf16[8,192,16]{1,2,0:T(8,128)(2,1)}, u32[]{:S(2)}) copy-start(bf16[8,192,16]{1,2,0:T(8,128)(2,1)} %param.34) | copy-start | bytes 147460
  45.1 317.2 %all-gather.15.cloned.1.call-start = ((), (), s32[]{:S(2)}) async-start(), calls=%async_computation.16 | async-start | bytes 1474560 | tf_op jit(solution)/shard_map/all_gather | solution.py:269
  45.9 119.1 %copy-start.77 = (bf16[8,192,16]{1,2,0:T(8,128)(2,1)S(1)}, bf16[8,192,16]{1,2,0:T(8,128)(2,1)}, u32[]{:S(2)}) copy-start(bf16[8,192,16]{1,2,0:T(8,128)(2,1)} %param.32) | copy-start | bytes 147460
  45.9 120.1 %copy-start.78 = (bf16[8,192,16]{1,2,0:T(8,128)(2,1)S(1)}, bf16[8,192,16]{1,2,0:T(8,128)(2,1)}, u32[]{:S(2)}) copy-start(bf16[8,192,16]{1,2,0:T(8,128)(2,1)} %param.30) | copy-start | bytes 147460
  171.6 56.4 %copy-start.91 = (s32[8,1]{0,1:T(1,128)S(1)}, s32[8,1]{0,1:T(1,128)}, u32[]{:S(2)}) copy-start(s32[8,1]{0,1:T(1,128)} %param.21) | copy-start | bytes 100
  256.5 81.9 %copy-start.79 = (bf16[8,16,192]{2,1,0:T(8,128)(2,1)S(1)}, bf16[8,16,192]{2,1,0:T(8,128)(2,1)}, u32[]{:S(2)}) copy-start(bf16[8,16,192]{2,1,0:T(8,128)(2,1)} %param.33) | copy-start | bytes 147460
  256.5 105.8 %all-to-all-start.1 = ((bf16[1225,4,576]{0,2,1:T(8,128)(2,1)}), bf16[1225,4,576]{0,2,1:T(8,128)(2,1)}, u32[]{:S(2)}, u32[]{:S(2)}) async-start(bf16[1225,4,576]{0,2,1:T(8,128)(2,1)} %bitcast.293), calls=%async_computation.1 | async-start | bytes 11796480 | tf_op jit(solution)/shard_map/all_to_all | solution.py:98
  261.8 91.5 %copy-start.93 = (u32[32]{0:T(128)S(1)}, u32[32]{0:T(128)}, u32[]{:S(2)}) copy-start(u32[32]{0:T(128)} %constant.173) | copy-start | bytes 388
  261.8 92.7 %copy-start.92 = (bf16[192]{0:T(256)(128)(2,1)S(1)}, bf16[192]{0:T(256)(128)(2,1)}, u32[]{:S(2)}) copy-start(bf16[192]{0:T(256)(128)(2,1)} %param.23) | copy-start | bytes 1156
  261.8 100.2 %copy-start.89 = (bf16[27,64]{1,0:T(8,128)(2,1)S(1)}, bf16[27,64]{1,0:T(8,128)(2,1)}, u32[]{:S(2)}) copy-start(bf16[27,64]{1,0:T(8,128)(2,1)} %param.29) | copy-start | bytes 10372
  261.9 572.0 %all-gather.11.cloned.1.call-start = ((), (), s32[]{:S(2)}) async-start(), calls=%async_computation.14 | async-start | bytes 1474560 | tf_op jit(solution)/shard_map/all_gather | solution.py:268
  262.6 571.3 %all-gather.9.cloned.1.call-start = ((), (), s32[]{:S(2)}) async-start(), calls=%async_computation.13 | async-start | bytes 1474560 | tf_op jit(solution)/shard_map/all_gather | solution.py:251
  338.4 590.4 %all-gather.17.cloned.1.call-start = ((), (), s32[]{:S(2)}) async-start(), calls=%async_computation.17 | async-start | bytes 5898240 | tf_op jit(solution)/shard_map/all_gather | solution.py:276
  362.0 190.1 %copy-start.63 = (bf16[14,14,64,1,1]{2,1,4,3,0:T(8,128)(2,1)}, bf16[14,14,64,1,1]{2,1,4,3,0:T(8,128)(2,1)S(1)}, u32[]{:S(2)}) copy-start(bf16[14,14,64,1,1]{2,1,4,3,0:T(8,128)(2,1)S(1)} %fusion.61) | copy-start | bytes 75268
  746.5 27.9 %all-to-all-start.2 = ((bf16[4,1225,192]{1,2,0:T(8,128)(2,1)}), bf16[4,1225,192]{1,2,0:T(8,128)(2,1)S(1)}, u32[]{:S(2)}, u32[]{:S(2)}) async-start(bf16[4,1225,192]{1,2,0:T(8,128)(2,1)} %copy.240), calls=%async_computation.2 | async-start | bytes 3932160 | tf_op jit(solution)/shard_map/all_to_all | solution.py:94
  775.7 70.0 %all-to-all-start.6 = ((bf16[4,1225,192]{1,2,0:T(8,128)(2,1)}), bf16[4,1225,192]{1,2,0:T(8,128)(2,1)S(1)}, u32[]{:S(2)}, u32[]{:S(2)}) async-start(bf16[4,1225,192]{1,2,0:T(8,128)(2,1)} %copy.253), calls=%async_computation.6 | async-start | bytes 3932160 | tf_op jit(solution)/shard_map/all_to_all | solution.py:82
  779.3 188.6 %all-gather.13.cloned.1.call-start = ((), (), s32[]{:S(2)}) async-start(), calls=%async_computation.15 | async-start | bytes 5898240 | tf_op jit(solution)/shard_map/all_gather | solution.py:275
  845.7 53.6 %all-to-all-start.3 = ((bf16[1225,4,192]{0,2,1:T(8,128)(2,1)}), bf16[1225,4,192]{0,2,1:T(8,128)(2,1)}, u32[]{:S(2)}, u32[]{:S(2)}) async-start(bf16[1225,4,192]{0,2,1:T(8,128)(2,1)} %bitcast.305), calls=%async_computation.3 | async-start | bytes 3932160 | tf_op jit(solution)/shard_map/all_to_all | solution.py:102
  867.8 149.5 %copy-start.55 = (bf16[1,3072,16]{1,2,0:T(8,128)(2,1)}, bf16[1,3072,16]{1,2,0:T(8,128)(2,1)S(1)}, u32[]{:S(2)}) copy-start(bf16[1,3072,16]{1,2,0:T(8,128)(2,1)S(1)} %copy.292) | copy-start | bytes 294916
  899.3 118.0 %copy-start.61 = (f32[1225,16]{0,1:T(8,128)}, f32[1225,16]{0,1:T(8,128)S(1)}, u32[]{:S(2)}) copy-start(f32[1225,16]{0,1:T(8,128)S(1)} %fusion.116) | copy-start | bytes 235204
  924.1 29.0 %all-to-all-start.4 = ((bf16[4,1225,192]{1,2,0:T(8,128)(2,1)}), bf16[4,1225,192]{1,2,0:T(8,128)(2,1)}, u32[]{:S(2)}, u32[]{:S(2)}) async-start(bf16[4,1225,192]{1,2,0:T(8,128)(2,1)} %copy.247), calls=%async_computation.4 | async-start | bytes 3932160 | tf_op jit(solution)/shard_map/all_to_all | solution.py:82
  1110.5 27.9 %all-to-all-start.8 = ((bf16[4,1225,192]{1,2,0:T(8,128)(2,1)}), bf16[4,1225,192]{1,2,0:T(8,128)(2,1)S(1)}, u32[]{:S(2)}, u32[]{:S(2)}) async-start(bf16[4,1225,192]{1,2,0:T(8,128)(2,1)} %copy.256), calls=%async_computation.8 | async-start | bytes 3932160 | tf_op jit(solution)/shard_map/all_to_all | solution.py:94
  1149.2 29.3 %all-to-all-start.9 = ((bf16[1225,4,192]{0,2,1:T(8,128)(2,1)}), bf16[1225,4,192]{0,2,1:T(8,128)(2,1)}, u32[]{:S(2)}, u32[]{:S(2)}) async-start(bf16[1225,4,192]{0,2,1:T(8,128)(2,1)} %bitcast.306), calls=%async_computation.9 | async-start | bytes 3932160 | tf_op jit(solution)/shard_map/all_to_all | solution.py:98
  1178.5 358.2 %all-to-all-start.5 = ((bf16[1225,4,192]{0,2,1:T(8,128)(2,1)}), bf16[1225,4,192]{0,2,1:T(8,128)(2,1)}, u32[]{:S(2)}, u32[]{:S(2)}) async-start(bf16[1225,4,192]{0,2,1:T(8,128)(2,1)} %bitcast.38), calls=%async_computation.5 | async-start | bytes 3932160 | tf_op jit(solution)/shard_map/all_to_all | solution.py:88
  1343.9 94.8 %copy-start.66 = (bf16[14,14,64]{2,1,0:T(8,128)(2,1)S(1)}, bf16[14,14,64]{2,1,0:T(8,128)(2,1)}, u32[]{:S(2)}) copy-start(bf16[14,14,64]{2,1,0:T(8,128)(2,1)} %copy-done.65) | copy-start | bytes 75268
  1536.7 72.1 %all-to-all-start.10 = ((bf16[4,1225,576]{1,2,0:T(8,128)(2,1)}), bf16[4,1225,576]{1,2,0:T(8,128)(2,1)}, u32[]{:S(2)}, u32[]{:S(2)}) async-start(bf16[4,1225,576]{1,2,0:T(8,128)(2,1)} %copy.270), calls=%async_computation.10 | async-start | bytes 11796480 | tf_op jit(solution)/shard_map/all_to_all | solution.py:94
  1627.2 33.6 %all-to-all-start.11 = ((bf16[1225,4,192]{0,2,1:T(8,128)(2,1)}), bf16[1225,4,192]{0,2,1:T(8,128)(2,1)}, u32[]{:S(2)}, u32[]{:S(2)}) async-start(bf16[1225,4,192]{0,2,1:T(8,128)(2,1)} %bitcast.304), calls=%async_computation.11 | async-start | bytes 3932160 | tf_op jit(solution)/shard_map/all_to_all | solution.py:102
  1631.8 174.2 %all-reduce.6.cloned.1.call-start = ((), (), s32[]{:S(2)}) async-start(), calls=%async_computation.18 | async-start | bytes 12582912 | tf_op jit(solution)/shard_map/psum | solution.py:326
  1689.6 130.2 %copy-start.1 = (bf16[27,64]{1,0:T(8,128)(2,1)S(1)}, bf16[27,64]{1,0:T(8,128)(2,1)}, u32[]{:S(2)}) copy-start(bf16[27,64]{1,0:T(8,128)(2,1)} %param.28) | copy-start | bytes 10372
  (84 other events, 808.3 us)
Sparse Core Ops, SparseCore 0:
  20.2 108.6 all-gather.6
  130.5 16.0 all-gather.14
  264.3 24.6 all-gather.10
  338.5 29.8 all-gather.8
  369.8 88.5 all-gather.16
  834.0 100.3 all-gather.12
  1643.3 162.6 all-reduce.5
where the time goes:
time: 1840 us; the launch traced here: 1830 us
  local copies, waits for them, and re-layouts  647 us (35%)
  blocking collectives  412 us (22%)
  matrix products  314 us (17%)
  waiting for transfers between devices  211 us (11%)
  other arithmetic  177 us (10%)
  starting transfers between devices  49.4 us (3%)
    add x6, local copies, waits for them, and re-layouts, score_matrix(): shaped + rel_rows[:, :, :, :, :, None] + rel_cols[:, :, :, :, None, :]  251 us
    all_gather x1, blocking collectives, body(): lax.all_gather(qkv_up, 'col', axis=2, tiled=True)  118 us
    psum x1, waiting for transfers between devices, body(): lax.psum((spread_pick(own_pick, qkv_pair[0]), spread_pick(own_pick, qkv_p...  107 us
    reshape x2, local copies, waits for them, and re-layouts, attend_back(): grad_s.astype(jnp.float32).reshape(windows, heads_local, WIN, WIN, WIN, WIN)  94.9 us
    reduce_sum x1, other arithmetic, attend_back(): along_rows = jnp.sum(split_grad, axis=5)  94.7 us
    all_gather x1, blocking collectives, body(): lax.all_gather(proj_weight, 'row', axis=1, tiled=True)  74.5 us
    all_to_all x4, waiting for transfers between devices, token_rows(): lax.all_to_all(values, 'row', split_axis=0, concat_axis=1, tiled=True)  65.1 us
    dot_general x4, matrix products, adapted_local(): jnp.dot(reduced, up_mat.astype(jnp.float32), precision=PRECISE)  53.4 us
  transfers between devices with their start and end apart: 18, of which 7 were waited for; matrix products, arithmetic and copies ran while one was open for 52% of the time, Pallas kernels for 0%

commit v1 on v0

--- a/solution.py
+++ b/solution.py
@@ -323,15 +323,14 @@
     grad_hidden_one = head_sums(adapted_back(grad_qkv_rows, qkv_full, qkv_dn, qkv_upm))
     qkv_pair = pair_grads(hidden_rows, grad_qkv_rows, qkv_dn, qkv_upm)
     proj_pair = pair_grads(attended_rows, grad_branch_rows, proj_dn, proj_upm)
-    attn_sums = lax.psum(
-        (
-            spread_pick(own_pick, qkv_pair[0]),
-            spread_pick(own_pick, qkv_pair[1]),
-            spread_pick(own_pick, proj_pair[0]),
-            spread_pick(own_pick, proj_pair[1]),
-        ),
-        ("dp", "row", "col"),
-    )
+    vals = (
+        spread_pick(own_pick, qkv_pair[0]),
+        spread_pick(own_pick, qkv_pair[1]),
+        spread_pick(own_pick, proj_pair[0]),
+        spread_pick(own_pick, proj_pair[1]),
+    )
+    passed = lax.psum(vals, axis_name=("row", "col"))
+    attn_sums = lax.psum(passed, axis_name="dp")
     qkv_down_grad = take_block(attn_sums[0], 1, row_index, qkv_down.shape[1])
     qkv_up_grad = take_block(attn_sums[1], 2, col_index, qkv_up.shape[2])
     proj_down_grad = take_block(attn_sums[2], 1, col_index, proj_down.shape[1])

time: 1840 us -> 1960 us (1.065)
  waiting for transfers between devices: 211 us -> 319 us
  blocking collectives: 412 us -> 440 us
    psum x1 -> x3, waiting for transfers between devices: 107 us -> 239 us  [the longest x1 111 us: body(): lax.psum((spread_pick(own_pick, fc1_local[0]), spread_pick(own_pick, fc1_...]
    all_to_all x0 -> x1, blocking collectives: none -> 26.9 us  [token_rows(): lax.all_to_all(values, 'row', split_axis=0, concat_axis=1, tiled=True)]
    all_to_all x4 -> x3, waiting for transfers between devices: 65.1 us -> 42.5 us  [token_rows(): lax.all_to_all(values, 'row', split_axis=0, concat_axis=1, tiled=True)]
  transfers between devices with their start and end apart: 18 -> 19, of which waited for: 7 -> 7; matrix products, arithmetic and copies ran while one was open for 52% -> 32% of each run, Pallas kernels for 0% -> 0%
where the time goes in v1:
time: 1960 us; the launch traced here: 1950 us
  local copies, waits for them, and re-layouts  646 us (33%)
  blocking collectives  440 us (22%)
  waiting for transfers between devices  319 us (16%)
  matrix products  311 us (16%)
  other arithmetic  173 us (9%)
  starting transfers between devices  42.9 us (2%)
    add x6, local copies, waits for them, and re-layouts, score_matrix(): shaped + rel_rows[:, :, :, :, :, None] + rel_cols[:, :, :, :, None, :]  252 us
    all_gather x1, blocking collectives, body(): lax.all_gather(qkv_up, 'col', axis=2, tiled=True)  118 us
    psum x1, waiting for transfers between devices, body(): lax.psum((spread_pick(own_pick, fc1_local[0]), spread_pick(own_pick, fc1_...  111 us
    reshape x2, local copies, waits for them, and re-layouts, attend_back(): grad_s.astype(jnp.float32).reshape(windows, heads_local, WIN, WIN, WIN, WIN)  95.1 us
    reduce_sum x1, other arithmetic, attend_back(): along_rows = jnp.sum(split_grad, axis=5)  94.7 us
    all_gather x1, blocking collectives, body(): lax.all_gather(proj_weight, 'row', axis=1, tiled=True)  74.6 us
    psum x1, waiting for transfers between devices, body(): attn_sums = lax.psum(passed, axis_name='dp')  64.1 us
    psum x1, waiting for transfers between devices, body(): passed = lax.psum(vals, axis_name=('row', 'col'))  63.1 us
  transfers between devices with their start and end apart: 19, of which 7 were waited for; matrix products, arithmetic and copies ran while one was open for 32% of the time, Pallas kernels for 0%

profile of v1, /device:TPU:0, one launch (start us, length us, event | category | flops | bytes accessed | tf_op | source)
XLA Modules:
  0.0 1948.6 jit_solution(17408236589304464791)
XLA Ops:
  46.6 118.0 %all_gather.54 = bf16[8,16,2304]{1,0,2:T(8,128)(2,1)} all-gather(bf16[8,16,576]{1,0,2:T(8,128)(2,1)S(1)} %copy.225), channel_id=1, replica_groups=mesh['dp'=2,'row'=4,'col'=4] {'col'}, dimensions={2}, use_global_device_ids=true | all-gather | bytes 737280 | tf_op jit(solution)/shard_map/all_gather | solution.py:252
  171.6 12.9 all_gather.62
  184.4 30.8 %all_gather.57 = bf16[8,768,16]{2,0,1:T(8,128)(2,1)S(1)} all-gather(bf16[8,192,16]{2,0,1:T(8,128)(2,1)} %copy.243), channel_id=1, replica_groups=mesh['dp'=2,'row'=4,'col'=4] {'col'}, dimensions={1}, use_global_device_ids=true | all-gather | bytes 245760 | tf_op jit(solution)/shard_map/all_gather | solution.py:253
  215.3 12.9 all_gather.53
  263.0 74.6 %all_gather.55 = bf16[192,768]{0,1:T(8,128)(2,1)S(1)} all-gather(bf16[192,192]{0,1:T(8,128)(2,1)S(1)} %copy.241), channel_id=1, replica_groups=mesh['dp'=2,'row'=4,'col'=4] {'row'}, dimensions={1}, use_global_device_ids=true | all-gather | bytes 368640 | tf_op jit(solution)/shard_map/all_gather | solution.py:245
  338.8 13.0 all_gather.58
  372.2 26.8 %reshape.211 = bf16[25,196,3,3,64]{1,0,4,3,2:T(8,128)(2,1)} reshape(bf16[4,1225,576]{1,0,2:T(4,128)(2,1)} %copy.227) | data formatting | bytes 11289600 | tf_op jit(solution)/shard_map/reshape | solution.py:142
  427.1 21.4 %add.279 = f32[25,3,14,14,14,14]{0,5,4,3,2,1:T(8,128)} broadcast(f32[25,3,14,14,14]{0,4,3,2,1:T(8,128)S(1)} %copy.236), dimensions={0,1,2,3,5} | broadcast | bytes 12348000 | tf_op jit(solution)/shard_map/add | solution.py:160
  448.5 64.5 %add.280 = f32[25,3,196,196]{0,3,2,1:T(8,128)} reshape(f32[25,3,14,14,14,14]{0,5,4,3,2,1:T(8,128)} %add.279) | data formatting | bytes 23049600 | tf_op jit(solution)/shard_map/add | solution.py:160
  513.0 39.2 %copy.237 = f32[25,3,196,196]{2,3,1,0:T(8,128)} copy(f32[25,3,196,196]{0,3,2,1:T(8,128)} %add.280) | data formatting | bytes 23049600 | tf_op jit(solution)/shard_map/add | solution.py:160
  563.4 22.8 %add.276 = f32[25,3,14,14,14,14]{0,5,4,3,2,1:T(8,128)} broadcast(f32[25,3,14,14,14]{0,4,3,2,1:T(8,128)} %copy.233), dimensions={0,1,2,3,4} | broadcast | bytes 12348000 | tf_op jit(solution)/shard_map/add | solution.py:160
  586.3 64.5 %add.277 = f32[25,3,196,196]{0,3,2,1:T(8,128)} reshape(f32[25,3,14,14,14,14]{0,5,4,3,2,1:T(8,128)} %add.276) | data formatting | bytes 23049600 | tf_op jit(solution)/shard_map/add | solution.py:160
  650.8 39.1 %copy.234 = f32[25,3,196,196]{2,3,1,0:T(8,128)} copy(f32[25,3,196,196]{0,3,2,1:T(8,128)} %add.277) | data formatting | bytes 23049600 | tf_op jit(solution)/shard_map/add | solution.py:160
  689.9 24.7 %fusion.132 = (f32[25,3,196]{2,1,0:T(4,128)S(1)}, f32[25,3,196,196]{2,3,1,0:T(8,128)}) fusion(f32[25,3,196,196]{2,3,1,0:T(8,128)} %copy.237, f32[25,3,196,196]{2,3,1,0:T(8,128)} %copy.234, bf16[25,196,3,1,64]{1,0,4,3,2:T(8,128)(2,1)} %get-tuple-element.41, bf16[25,196,3,1,64]{1,0,4,3,2:T(8,128)(2,1)S(1)} %copy-done.9), kind=kOutput, calls=%fused_computation.234 | convolution fusion | flops 380303744 | bytes 38396400 | tf_op jit(solution)/shard_map/nqhc,nkhc->nhqk/dot_general | solution.py:149
  779.2 33.6 %all_gather.67 = bf16[8,16,768]{1,0,2:T(8,128)(2,1)S(1)} all-gather(bf16[8,16,192]{1,0,2:T(8,128)(2,1)} %copy.250), channel_id=1, replica_groups=mesh['dp'=2,'row'=4,'col'=4] {'row'}, dimensions={2}, use_global_device_ids=true | all-gather | bytes 245760 | tf_op jit(solution)/shard_map/all_gather | solution.py:271
  814.4 19.3 all_gather.66
  868.2 30.2 %all_gather.63 = bf16[8,16,3072]{2,1,0:T(8,128)(2,1)S(1)} all-gather(bf16[8,16,768]{2,1,0:T(8,128)(2,1)S(1)} %copy-done.74), channel_id=1, replica_groups=mesh['dp'=2,'row'=4,'col'=4] {'col'}, dimensions={2}, use_global_device_ids=true | all-gather | bytes 983040 | tf_op jit(solution)/shard_map/all_gather | solution.py:277
  940.7 12.5 all-to-all-done.4
  976.0 41.4 %multiply_convert_fusion.1 = (bf16[1225,3072]{1,0:T(8,128)(2,1)}, f32[1225,3072]{1,0:T(8,128)}, f32[1225,3072]{1,0:T(8,128)}) fusion(f32[1225,3072]{1,0:T(8,128)S(1)} %fusion.135, f32[1225,16]{0,1:T(8,128)S(1)} %fusion.149, bf16[1,16,3072]{2,0,1:T(2,128)(2,1)S(1)} %fusion.64), kind=kOutput, calls=%fused_computation.9 | convolution fusion | flops 970905600 | bytes 52861504 | tf_op jit(solution)/shard_map/dot_general | solution.py:110
  1017.4 22.8 %add_convert_fusion = bf16[1225,3072]{1,0:T(8,128)(2,1)} fusion(f32[1225,3072]{1,0:T(8,128)} %get-tuple-element.36, f32[1225,3072]{1,0:T(8,128)} %fusion.137, f32[1225,3072]{1,0:T(8,128)} %get-tuple-element.55, f32[1225,16]{0,1:T(8,128)S(1)} %fusion.116, bf16[1,3072,16]{1,2,0:T(8,128)(2,1)S(1)} %copy.292), kind=kOutput, calls=%fused_computation.8 | convolution fusion | flops 778982400 | bytes 52861504 | tf_op jit(solution)/shard_map/dot_general | solution.py:117
  1062.6 27.2 %all_to_all.186 = bf16[1225,4,192]{0,2,1:T(8,128)(2,1)S(1)} all-to-all(bf16[1225,4,192]{0,2,1:T(8,128)(2,1)S(1)} %bitcast.307), channel_id=1, replica_groups=mesh['dp'=2,'row'=4,'col'=4] {'row'}, dimensions={1} | all-to-all | bytes 3763200 | tf_op jit(solution)/shard_map/all_to_all | solution.py:88
  1109.3 26.9 %all_to_all.187 = bf16[4,1225,192]{1,2,0:T(8,128)(2,1)S(1)} all-to-all(bf16[4,1225,192]{1,2,0:T(8,128)(2,1)S(1)} %copy.256), channel_id=1, replica_groups=mesh['dp'=2,'row'=4,'col'=4] {'row'}, dimensions={0} | all-to-all | bytes 3763200 | tf_op jit(solution)/shard_map/all_to_all | solution.py:94
  1146.3 24.2 %all-to-all-done.9 = bf16[1225,4,192]{0,2,1:T(8,128)(2,1)S(1)} async-done(((bf16[1225,4,192]{0,2,1:T(8,128)(2,1)}), bf16[1225,4,192]{0,2,1:T(8,128)(2,1)S(1)}, u32[]{:S(2)}, u32[]{:S(2)}) %all-to-all-start.9) | async-done | bytes 1881632 | tf_op jit(solution)/shard_map/all_to_all | solution.py:98
  1193.7 21.8 %multiply_reduce_fusion = (f32[25,3,196]{2,1,0:T(4,128)S(1)}, f32[25,3,196,196]{2,3,1,0:T(8,128)}) fusion(f32[25,3,196,196]{2,3,1,0:T(8,128)} %get-tuple-element.54, f32[25,3,196]{2,1,0:T(4,128)S(1)} %log_add_fusion, bf16[25,196,3,1,64]{1,0,4,3,2:T(8,128)(2,1)} %get-tuple-element.39, bf16[25,196,3,64]{1,0,3,2:T(8,128)(2,1)S(1)} %reshape.212), kind=kOutput, calls=%fused_computation.2 | convolution fusion | flops 377422528 | bytes 26930400 | tf_op jit(solution)/shard_map/nqhc,nkhc->nhqk/dot_general | solution.py:185
  1234.6 30.4 %copy.261 = f32[25,3,196,196]{0,3,2,1:T(8,128)} copy(bf16[25,3,196,196]{2,3,1,0:T(8,128)(2,1)} %copy-done.2) | data formatting | bytes 17287200 | tf_op jit(solution)/shard_map/reshape | solution.py:194
  1264.9 64.7 %reshape.221 = f32[25,3,14,14,14,14]{0,5,4,3,2,1:T(8,128)} reshape(f32[25,3,196,196]{0,3,2,1:T(8,128)} %copy.261) | data formatting | bytes 23049600 | tf_op jit(solution)/shard_map/reshape | solution.py:194
  1329.7 94.7 %fusion.128 = (f32[25,3,14,14,14]{0,4,3,2,1:T(8,128)}, f32[25,3,14,14,14]{0,4,3,2,1:T(8,128)}) fusion(f32[25,3,14,14,14,14]{0,5,4,3,2,1:T(8,128)} %reshape.221), kind=kLoop, calls=%fused_computation.231 | loop fusion | flops 5350800 | bytes 13171200 | tf_op jit(solution)/shard_map/reduce_sum | solution.py:195
  1492.2 24.3 %convert_element_type.249 = bf16[4,1225,576]{1,0,2:T(4,128)(2,1)} reshape(bf16[25,196,3,3,64]{1,0,4,3,2:T(8,128)(2,1)} %copy.269) | data formatting | bytes 11289600 | tf_op jit(solution)/shard_map/convert_element_type | solution.py:205
  1562.5 32.0 %all-to-all-done.10 = bf16[4,1225,576]{1,2,0:T(8,128)(2,1)} async-done(((bf16[4,1225,576]{1,2,0:T(8,128)(2,1)}), bf16[4,1225,576]{1,2,0:T(8,128)(2,1)}, u32[]{:S(2)}, u32[]{:S(2)}) %all-to-all-start.10) | async-done | bytes 5644832 | tf_op jit(solution)/shard_map/all_to_all | solution.py:94
  1652.8 63.1 %all-reduce.12.cloned.1.call-done = (f32[8,768,16]{1,2,0:T(8,128)}, f32[8,16,2304]{2,1,0:T(8,128)}, f32[8,768,16]{1,2,0:T(8,128)}, f32[8,16,768]{2,1,0:T(8,128)}) async-done(((f32[8,768,16]{1,2,0:T(8,128)}, f32[8,16,2304]{2,1,0:T(8,128)}, f32[8,768,16]{1,2,0:T(8,128)}, f32[8,16,768]{2,1,0:T(8,128)}), (f32[8,768,16]{1,2,0:T(8,128)}, f32[8,16,2304]{2,1,0:T(8,128)}, f32[8,768,16]{1,2,0:T(8,128)}, ...) | async-done | bytes 2359312 | tf_op jit(solution)/shard_map/psum | solution.py:332
  1752.2 111.4 %all-reduce.10.cloned.1.call-done = (f32[8,768,16]{1,2,0:T(8,128)}, f32[8,16,3072]{2,1,0:T(8,128)}, f32[8,3072,16]{1,2,0:T(8,128)}, f32[8,16,768]{2,1,0:T(8,128)}) async-done(((f32[8,768,16]{1,2,0:T(8,128)}, f32[8,16,3072]{2,1,0:T(8,128)}, f32[8,3072,16]{1,2,0:T(8,128)}, f32[8,16,768]{2,1,0:T(8,128)}), (f32[8,768,16]{1,2,0:T(8,128)}, f32[8,16,3072]{2,1,0:T(8,128)}, f32[8,3072,16]{1,2,0:T(8,128)}, ...) | async-done | bytes 3932176 | tf_op jit(solution)/shard_map/psum | solution.py:302
  1870.6 64.1 %all-reduce.14.cloned.1.call-done = (f32[8,768,16]{1,2,0:T(8,128)}, f32[8,16,2304]{2,1,0:T(8,128)}, f32[8,768,16]{1,2,0:T(8,128)}, f32[8,16,768]{2,1,0:T(8,128)}) async-done(((f32[8,768,16]{1,2,0:T(8,128)}, f32[8,16,2304]{2,1,0:T(8,128)}, f32[8,768,16]{1,2,0:T(8,128)}, f32[8,16,768]{2,1,0:T(8,128)}), (f32[8,768,16]{1,2,0:T(8,128)}, f32[8,16,2304]{2,1,0:T(8,128)}, f32[8,768,16]{1,2,0:T(8,128)}, ...) | async-done | bytes 2359312 | tf_op jit(solution)/shard_map/psum | solution.py:333
  (388 shorter events, 622.3 us)
Async XLA Ops:
  7.2 354.7 %copy-start = (bf16[27,64]{1,0:T(8,128)(2,1)S(1)}, bf16[27,64]{1,0:T(8,128)(2,1)}, u32[]{:S(2)}) copy-start(bf16[27,64]{1,0:T(8,128)(2,1)} %param.28) | copy-start | bytes 10372
  7.2 226.0 %all-gather.7.cloned.1.call-start = ((), (), s32[]{:S(2)}) async-start(), calls=%async_computation.12 | async-start | bytes 4423680 | tf_op jit(solution)/shard_map/all_gather | solution.py:250
  41.4 191.4 %all-to-all-start = ((bf16[4,1225,192]{1,2,0:T(8,128)(2,1)}), bf16[4,1225,192]{1,2,0:T(8,128)(2,1)S(1)}, u32[]{:S(2)}, u32[]{:S(2)}) async-start(bf16[4,1225,192]{1,2,0:T(8,128)(2,1)} %copy.222), calls=%async_computation | async-start | bytes 3932160 | tf_op jit(solution)/shard_map/all_to_all | solution.py:94
  45.0 119.7 %copy-start.77 = (bf16[8,192,16]{1,2,0:T(8,128)(2,1)S(1)}, bf16[8,192,16]{1,2,0:T(8,128)(2,1)}, u32[]{:S(2)}) copy-start(bf16[8,192,16]{1,2,0:T(8,128)(2,1)} %param.34) | copy-start | bytes 147460
  45.0 317.4 %all-gather.15.cloned.1.call-start = ((), (), s32[]{:S(2)}) async-start(), calls=%async_computation.16 | async-start | bytes 1474560 | tf_op jit(solution)/shard_map/all_gather | solution.py:269
  45.8 119.1 %copy-start.78 = (bf16[8,192,16]{1,2,0:T(8,128)(2,1)S(1)}, bf16[8,192,16]{1,2,0:T(8,128)(2,1)}, u32[]{:S(2)}) copy-start(bf16[8,192,16]{1,2,0:T(8,128)(2,1)} %param.32) | copy-start | bytes 147460
  45.8 120.1 %copy-start.79 = (bf16[8,192,16]{1,2,0:T(8,128)(2,1)S(1)}, bf16[8,192,16]{1,2,0:T(8,128)(2,1)}, u32[]{:S(2)}) copy-start(bf16[8,192,16]{1,2,0:T(8,128)(2,1)} %param.30) | copy-start | bytes 147460
  256.6 81.9 %copy-start.80 = (bf16[8,16,192]{2,1,0:T(8,128)(2,1)S(1)}, bf16[8,16,192]{2,1,0:T(8,128)(2,1)}, u32[]{:S(2)}) copy-start(bf16[8,16,192]{2,1,0:T(8,128)(2,1)} %param.33) | copy-start | bytes 147460
  256.6 105.8 %all-to-all-start.1 = ((bf16[1225,4,576]{0,2,1:T(8,128)(2,1)}), bf16[1225,4,576]{0,2,1:T(8,128)(2,1)}, u32[]{:S(2)}, u32[]{:S(2)}) async-start(bf16[1225,4,576]{0,2,1:T(8,128)(2,1)} %bitcast.291), calls=%async_computation.1 | async-start | bytes 11796480 | tf_op jit(solution)/shard_map/all_to_all | solution.py:98
  261.9 91.5 %copy-start.94 = (u32[32]{0:T(128)S(1)}, u32[32]{0:T(128)}, u32[]{:S(2)}) copy-start(u32[32]{0:T(128)} %constant.173) | copy-start | bytes 388
  261.9 92.7 %copy-start.93 = (bf16[192]{0:T(256)(128)(2,1)S(1)}, bf16[192]{0:T(256)(128)(2,1)}, u32[]{:S(2)}) copy-start(bf16[192]{0:T(256)(128)(2,1)} %param.23) | copy-start | bytes 1156
  262.0 100.2 %copy-start.90 = (bf16[27,64]{1,0:T(8,128)(2,1)S(1)}, bf16[27,64]{1,0:T(8,128)(2,1)}, u32[]{:S(2)}) copy-start(bf16[27,64]{1,0:T(8,128)(2,1)} %param.29) | copy-start | bytes 10372
  262.0 571.8 %all-gather.11.cloned.1.call-start = ((), (), s32[]{:S(2)}) async-start(), calls=%async_computation.14 | async-start | bytes 1474560 | tf_op jit(solution)/shard_map/all_gather | solution.py:268
  262.7 571.1 %all-gather.9.cloned.1.call-start = ((), (), s32[]{:S(2)}) async-start(), calls=%async_computation.13 | async-start | bytes 1474560 | tf_op jit(solution)/shard_map/all_gather | solution.py:251
  338.5 590.4 %all-gather.17.cloned.1.call-start = ((), (), s32[]{:S(2)}) async-start(), calls=%async_computation.17 | async-start | bytes 5898240 | tf_op jit(solution)/shard_map/all_gather | solution.py:276
  362.1 190.0 %copy-start.66 = (bf16[14,14,64,1,1]{2,1,4,3,0:T(8,128)(2,1)}, bf16[14,14,64,1,1]{2,1,4,3,0:T(8,128)(2,1)S(1)}, u32[]{:S(2)}) copy-start(bf16[14,14,64,1,1]{2,1,4,3,0:T(8,128)(2,1)S(1)} %fusion.61) | copy-start | bytes 75268
  746.4 27.9 %all-to-all-start.2 = ((bf16[4,1225,192]{1,2,0:T(8,128)(2,1)}), bf16[4,1225,192]{1,2,0:T(8,128)(2,1)S(1)}, u32[]{:S(2)}, u32[]{:S(2)}) async-start(bf16[4,1225,192]{1,2,0:T(8,128)(2,1)} %copy.240), calls=%async_computation.2 | async-start | bytes 3932160 | tf_op jit(solution)/shard_map/all_to_all | solution.py:94
  775.6 70.0 %all-to-all-start.6 = ((bf16[4,1225,192]{1,2,0:T(8,128)(2,1)}), bf16[4,1225,192]{1,2,0:T(8,128)(2,1)S(1)}, u32[]{:S(2)}, u32[]{:S(2)}) async-start(bf16[4,1225,192]{1,2,0:T(8,128)(2,1)} %copy.253), calls=%async_computation.6 | async-start | bytes 3932160 | tf_op jit(solution)/shard_map/all_to_all | solution.py:82
  779.2 188.8 %all-gather.13.cloned.1.call-start = ((), (), s32[]{:S(2)}) async-start(), calls=%async_computation.15 | async-start | bytes 5898240 | tf_op jit(solution)/shard_map/all_gather | solution.py:275
  845.6 53.9 %all-to-all-start.3 = ((bf16[1225,4,192]{0,2,1:T(8,128)(2,1)}), bf16[1225,4,192]{0,2,1:T(8,128)(2,1)}, u32[]{:S(2)}, u32[]{:S(2)}) async-start(bf16[1225,4,192]{0,2,1:T(8,128)(2,1)} %bitcast.304), calls=%async_computation.3 | async-start | bytes 3932160 | tf_op jit(solution)/shard_map/all_to_all | solution.py:102
  868.0 149.4 %copy-start.58 = (bf16[1,3072,16]{1,2,0:T(8,128)(2,1)}, bf16[1,3072,16]{1,2,0:T(8,128)(2,1)S(1)}, u32[]{:S(2)}) copy-start(bf16[1,3072,16]{1,2,0:T(8,128)(2,1)S(1)} %copy.292) | copy-start | bytes 294916
  899.4 117.9 %copy-start.64 = (f32[1225,16]{0,1:T(8,128)}, f32[1225,16]{0,1:T(8,128)S(1)}, u32[]{:S(2)}) copy-start(f32[1225,16]{0,1:T(8,128)S(1)} %fusion.116) | copy-start | bytes 235204
  924.2 29.0 %all-to-all-start.4 = ((bf16[4,1225,192]{1,2,0:T(8,128)(2,1)}), bf16[4,1225,192]{1,2,0:T(8,128)(2,1)}, u32[]{:S(2)}, u32[]{:S(2)}) async-start(bf16[4,1225,192]{1,2,0:T(8,128)(2,1)} %copy.247), calls=%async_computation.4 | async-start | bytes 3932160 | tf_op jit(solution)/shard_map/all_to_all | solution.py:82
  1142.4 28.0 %all-to-all-start.9 = ((bf16[1225,4,192]{0,2,1:T(8,128)(2,1)}), bf16[1225,4,192]{0,2,1:T(8,128)(2,1)S(1)}, u32[]{:S(2)}, u32[]{:S(2)}) async-start(bf16[1225,4,192]{0,2,1:T(8,128)(2,1)} %bitcast.306), calls=%async_computation.9 | async-start | bytes 3932160 | tf_op jit(solution)/shard_map/all_to_all | solution.py:98
  1329.7 94.8 %copy-start.69 = (bf16[14,14,64]{2,1,0:T(8,128)(2,1)S(1)}, bf16[14,14,64]{2,1,0:T(8,128)(2,1)}, u32[]{:S(2)}) copy-start(bf16[14,14,64]{2,1,0:T(8,128)(2,1)} %copy-done.68) | copy-start | bytes 75268
  1522.5 71.9 %all-to-all-start.10 = ((bf16[4,1225,576]{1,2,0:T(8,128)(2,1)}), bf16[4,1225,576]{1,2,0:T(8,128)(2,1)}, u32[]{:S(2)}, u32[]{:S(2)}) async-start(bf16[4,1225,576]{1,2,0:T(8,128)(2,1)} %copy.270), calls=%async_computation.10 | async-start | bytes 11796480 | tf_op jit(solution)/shard_map/all_to_all | solution.py:94
  1594.5 40.9 %all-to-all-start.5 = ((bf16[1225,4,192]{0,2,1:T(8,128)(2,1)}), bf16[1225,4,192]{0,2,1:T(8,128)(2,1)S(1)}, u32[]{:S(2)}, u32[]{:S(2)}) async-start(bf16[1225,4,192]{0,2,1:T(8,128)(2,1)} %bitcast.302), calls=%async_computation.5 | async-start | bytes 3932160 | tf_op jit(solution)/shard_map/all_to_all | solution.py:88
  1598.1 117.9 %all-reduce.12.cloned.1.call-start = ((), (), s32[]{:S(2)}) async-start(), calls=%async_computation.19 | async-start | bytes 4718592 | tf_op jit(solution)/shard_map/psum | solution.py:332
  1613.4 250.2 %all-reduce.10.cloned.1.call-start = ((), (), s32[]{:S(2)}) async-start(), calls=%async_computation.18 | async-start | bytes 7864320 | tf_op jit(solution)/shard_map/psum | solution.py:302
  1636.7 79.3 %all-to-all-start.11 = ((bf16[1225,4,192]{0,2,1:T(8,128)(2,1)}), bf16[1225,4,192]{0,2,1:T(8,128)(2,1)S(1)}, u32[]{:S(2)}, u32[]{:S(2)}) async-start(bf16[1225,4,192]{0,2,1:T(8,128)(2,1)} %bitcast.303), calls=%async_computation.11 | async-start | bytes 3932160 | tf_op jit(solution)/shard_map/all_to_all | solution.py:102
  1640.3 294.4 %all-reduce.14.cloned.1.call-start = ((), (), s32[]{:S(2)}) async-start(), calls=%async_computation.20 | async-start | bytes 4718592 | tf_op jit(solution)/shard_map/psum | solution.py:333
  1742.5 199.1 %copy-start.1 = (bf16[27,64]{1,0:T(8,128)(2,1)S(1)}, bf16[27,64]{1,0:T(8,128)(2,1)}, u32[]{:S(2)}) copy-start(bf16[27,64]{1,0:T(8,128)(2,1)} %param.28) | copy-start | bytes 10372
  (84 other events, 832.7 us)
Sparse Core Ops, SparseCore 0:
  20.2 108.7 all-gather.6
  130.5 16.0 all-gather.14
  264.4 24.7 all-gather.10
  338.6 29.9 all-gather.8
  370.0 88.5 all-gather.16
  833.9 100.4 all-gather.12
  1613.6 102.3 all-reduce.11
  1722.6 141.0 all-reduce.9
  1866.3 68.3 all-reduce.13
